TPU v7x, 32 devices: a whole 2x2x4 slice. The times are simulated.
32 devices in a mesh: outer: 8 (over z, y), narrow: 4 (over x, core).
Axes of the slice: x: 2, y: 2, z: 4, core: 2. Of those that a mesh axis runs over, the one named last changes fastest.
Arguments:
- queries: bfloat16 [8192, 4096], P(('outer', 'narrow')), may hold values from -6 to 6
- keys: bfloat16 [8192, 4096], P(('outer', 'narrow')), may hold values from -6 to 6
- values: bfloat16 [8192, 4096], P(('outer', 'narrow')), may hold values from -6 to 6
- log_decay: float32 [32, 8192], P(None, ('outer', 'narrow')), may hold values from -0.8 to 0
- gain: float32 [4096], replicated, may hold values from 0.5 to 1.5
Outputs:
- mixed: bfloat16 [8192, 4096], P(('outer', 'narrow'))
All inputs are finite; a program needn't handle non-finite values.
Results may differ from a plain program's by a relative error of at most 0.0052.
Values may be sent and summed in bfloat16 or wider, within the bound.
A program may use at most 64 MiB of HBM per device.

v0:
```python
import math

import jax
import jax.numpy as jnp
from jax import lax
from jax.sharding import PartitionSpec as P


def entering(shard, axis, combine, identity):
    devices, position = (lax.axis_size(axis), lax.axis_index(axis))
    everything = jax.tree.map(lambda part: lax.all_gather(part, axis), shard)
    start = jax.tree.map(
        lambda part, zero: jnp.broadcast_to(jnp.asarray(zero, part.dtype), part.shape),
        shard,
        identity,
    )

    def hop(k, before):
        reached = k < position
        new = combine(before, jax.tree.map(lambda part: part[k], everything))
        return jax.tree.map(lambda a, b: jnp.where(reached, a, b), new, before)

    return lax.fori_loop(0, devices, hop, start)


def combine(earlier, later):
    return (earlier[0] + later[0], jnp.exp(later[0])[:, None, None] * earlier[1] + later[1])


def group_prefix(totals, states):
    start = (jnp.zeros(totals.shape[1:], jnp.float32), jnp.zeros(states.shape[1:], jnp.float32))

    def advance(carry, item):
        return (combine(carry, item), carry)

    whole, before = lax.scan(advance, start, (totals, states))
    return (whole, before)


def on_device(queries, keys, values, log_decay, gain):
    tokens = queries.shape[0]
    heads = log_decay.shape[0]
    width = queries.shape[1] // heads
    qthree = queries.reshape(tokens, heads, width)
    kthree = keys.reshape(tokens, heads, width)
    vthree = values.reshape(tokens, heads, width)
    cum = jnp.cumsum(log_decay, axis=1)
    total = cum[:, -1]
    factor = jnp.exp(total[:, None] - cum).T
    decayed = (kthree.astype(jnp.float32) * factor[:, :, None]).astype(jnp.bfloat16)
    block_state = jnp.einsum("thd,the->hde", decayed, vthree, preferred_element_type=jnp.float32)
    moved_states, moved_totals = (
        lax.all_to_all(block_state[None], "narrow", split_axis=1, concat_axis=0, tiled=True),
        lax.all_to_all(total[None], "narrow", split_axis=1, concat_axis=0, tiled=True),
    )
    whole, before = group_prefix(moved_totals, moved_states)
    owned = moved_totals.shape[1]
    identity = (jnp.zeros((owned,), jnp.float32), jnp.zeros((owned, width, width), jnp.float32))
    earlier = entering(whole, "outer", combine, identity)
    prefix = jnp.exp(before[0])[:, :, None, None] * earlier[1][None] + before[1]
    back = lax.all_to_all(
        prefix.astype(jnp.bfloat16), "narrow", split_axis=0, concat_axis=1, tiled=True
    )
    carried_half = back.reshape(heads, width, width)
    causal = jnp.arange(tokens)[:, None] >= jnp.arange(tokens)[None, :]
    group = math.gcd(heads, 8)
    pieces = []
    for first in range(0, heads, group):
        qpart = qthree[:, first : first + group]
        kpart = kthree[:, first : first + group]
        vpart = vthree[:, first : first + group]
        running_partial = cum[first : first + group]
        scores = jnp.einsum("thd,shd->hts", qpart, kpart, preferred_element_type=jnp.float32)
        spread = jnp.minimum(running_partial[:, :, None] - running_partial[:, None, :], 0.0)
        weights = jnp.where(causal[None], scores * jnp.exp(spread), 0.0).astype(jnp.bfloat16)
        inner = jnp.einsum("hts,she->the", weights, vpart, preferred_element_type=jnp.float32)
        readout = jnp.einsum(
            "thd,hde->the",
            qpart,
            carried_half[first : first + group],
            preferred_element_type=jnp.float32,
        )
        pieces.append(inner + readout * jnp.exp(running_partial).T[:, :, None])
    numer = jnp.concatenate(pieces, axis=1)
    scale = lax.rsqrt(jnp.mean(numer * numer, axis=-1, keepdims=True) + 1e-06)
    result = numer * scale * gain.reshape(heads, width)[None]
    return result.astype(jnp.bfloat16).reshape(tokens, heads * width)


def solution(mesh):
    in_specs = (
        P(("outer", "narrow"), None),
        P(("outer", "narrow"), None),
        P(("outer", "narrow"), None),
        P(None, ("outer", "narrow")),
        P(),
    )
    out_specs = P(("outer", "narrow"), None)
    return jax.shard_map(
        on_device, mesh=mesh, in_specs=in_specs, out_specs=out_specs, check_vma=False
    )
```

profile of v0, /device:TPU:1, one launch (start us, length us, event | category | flops | bytes accessed | tf_op | source)
XLA Modules:
  0.0 197.3 jit_solution(6226211713675117474)
XLA Ops:
  9.0 4.3 %all-to-all-start = ((f32[1,4,8]{2,0,1:T(1,128)}), f32[1,4,8]{2,0,1:T(1,128)S(1)}, u32[]{:S(2)}, u32[]{:S(2)}) async-start(f32[1,4,8]{2,0,1:T(1,128)} %bitcast.5), calls=%async_computation | async-start | bytes 4096 | tf_op jit(solution)/shard_map/all_to_all | solution.py:54
  13.4 4.1 %copy.59 = bf16[256,4096]{0,1:T(8,128)(2,1)} copy(bf16[256,4096]{1,0:T(8,128)(2,1)} %param.10) | data formatting | bytes 4194304 | tf_op args[1]
  17.5 3.3 %copy.62 = bf16[256,4096]{0,1:T(8,128)(2,1)S(1)} copy(bf16[256,4096]{1,0:T(8,128)(2,1)} %param.11) | data formatting | bytes 4194304 | tf_op args[2]
  20.7 3.6 %fusion.8 = f32[1,32,128,128]{3,2,0,1:T(8,128)} fusion(bf16[256,32,128]{0,2,1:T(8,128)(2,1)S(1)} %bitcast.131, bf16[256,32,128]{0,2,1:T(8,128)(2,1)} %bitcast.137, f32[256,32]{0,1:T(8,128)S(1)} %exponential_bitcast_fusion.1), kind=kOutput, calls=%fused_computation.24 | convolution fusion | flops 271581184 | bytes 6324224 | tf_op jit(solution)/shard_map/thd,the->hde/dot_general | solution.py:51
  24.4 4.4 %all-to-all-start.1 = ((f32[1,32,128,128]{3,2,0,1:T(8,128)}), f32[1,32,128,128]{3,2,0,1:T(8,128)}, u32[]{:S(2)}, u32[]{:S(2)}) async-start(f32[1,32,128,128]{3,2,0,1:T(8,128)} %fusion.8), calls=%async_computation.1 | async-start | bytes 4194304 | tf_op jit(solution)/shard_map/all_to_all | solution.py:53
  28.9 24.7 %all-to-all-done.1 = f32[1,32,128,128]{3,2,0,1:T(8,128)} async-done(((f32[1,32,128,128]{3,2,0,1:T(8,128)}), f32[1,32,128,128]{3,2,0,1:T(8,128)}, u32[]{:S(2)}, u32[]{:S(2)}) %all-to-all-start.1) | async-done | bytes 2097184 | tf_op jit(solution)/shard_map/all_to_all | solution.py:53
  53.6 12.7 %while.31 = (s32[]{:T(128)}, f32[8]{0:T(128)S(1)}, f32[8,128,128]{2,1,0:T(8,128)}, f32[4,8]{1,0:T(4,128)S(1)}, f32[4,8,128,128]{2,3,1,0:T(8,128)}, /*index=5*/f3...) while((s32[]{:T(128)}, f32[8]{0:T(128)S(1)}, f32[8,128,128]{2,1,0:T(8,128)}, ...), condition=%wide.region_3.4_spmd.clone, body=%wide.region_2.3_spmd.clone.sunk | while | flops 393235 | bytes 4195188 | solution.py:36
  53.6 1.9 select_bitcast_fusion.2
  56.6 2.1 %select_bitcast_fusion.2 = (f32[1,8,128,128]{3,2,1,0:T(8,128)S(1)}, f32[8,128,128]{2,1,0:T(8,128)}) fusion(f32[8,128,128]{2,1,0:T(8,128)} %get-tuple-element.318, pred[]{:T(512)S(6)} %compare.6, f32[4,8,128,128]{3,2,1,0:T(8,128)} %get-tuple-element.331, s32[]{:T(128)} %get-tuple-element.316, f32[8]{0:T(128)S(1)} %get-tuple-element.298), kind=kLoop, calls=%fused_computation.1.clone.1 | loop fusion | flops 393216 | bytes 2097189 | tf_op jit(solution)/shard_map/while/body/jit(dynamic_update_index_in_dim)/broadcast_in_dim | solution.py:36
  59.9 2.1 %select_bitcast_fusion.2 = (f32[1,8,128,128]{3,2,1,0:T(8,128)S(1)}, f32[8,128,128]{2,1,0:T(8,128)}) fusion(f32[8,128,128]{2,1,0:T(8,128)} %get-tuple-element.318, pred[]{:T(512)S(6)} %compare.6, f32[4,8,128,128]{3,2,1,0:T(8,128)} %get-tuple-element.331, s32[]{:T(128)} %get-tuple-element.316, f32[8]{0:T(128)S(1)} %get-tuple-element.298), kind=kLoop, calls=%fused_computation.1.clone.1 | loop fusion | flops 393216 | bytes 2097189 | tf_op jit(solution)/shard_map/while/body/jit(dynamic_update_index_in_dim)/broadcast_in_dim | solution.py:36
  63.1 2.1 %select_bitcast_fusion.2 = (f32[1,8,128,128]{3,2,1,0:T(8,128)S(1)}, f32[8,128,128]{2,1,0:T(8,128)}) fusion(f32[8,128,128]{2,1,0:T(8,128)} %get-tuple-element.318, pred[]{:T(512)S(6)} %compare.6, f32[4,8,128,128]{3,2,1,0:T(8,128)} %get-tuple-element.331, s32[]{:T(128)} %get-tuple-element.316, f32[8]{0:T(128)S(1)} %get-tuple-element.298), kind=kLoop, calls=%fused_computation.1.clone.1 | loop fusion | flops 393216 | bytes 2097189 | tf_op jit(solution)/shard_map/while/body/jit(dynamic_update_index_in_dim)/broadcast_in_dim | solution.py:36
  66.3 4.1 %copy.57 = bf16[256,4096]{0,1:T(8,128)(2,1)} copy(bf16[256,4096]{1,0:T(8,128)(2,1)} %param.9) | data formatting | bytes 4194304 | tf_op args[0]
  71.7 2.1 %select_convert_fusion.3 = bf16[8,256,256]{2,1,0:T(8,128)(2,1)S(1)} fusion(bf16[256,32,128]{0,2,1:T(8,128)(2,1)} %bitcast.142, f32[8,256]{1,0:T(8,128)S(1)} %get-tuple-element.219, pred[256,256]{1,0:T(8,128)(4,1)S(1)} %iota_compare_fusion, bf16[256,32,128]{0,2,1:T(8,128)(2,1)} %bitcast.138), kind=kOutput, calls=%fused_computation.23 | convolution fusion | flops 136839168 | bytes 3751936 | tf_op jit(solution)/shard_map/thd,shd->hts/dot_general | solution.py:73
  73.8 1.5 convolution_bitcast_fusion.7
  76.7 1.5 convolution_bitcast_fusion.6
  78.9 1.5 convolution_bitcast_fusion.5
  80.7 18.9 %all-reduce = f32[64]{0:T(128)S(1)} all-reduce(f32[64]{0:T(128)S(1)} %dynamic-update-slice), channel_id=2, replica_groups=mesh['outer'=8,'narrow'=4] {'outer'}, use_global_device_ids=true, to_apply=%add | all-reduce | flops 64 | bytes 512
  99.7 39.8 %all-gather.4.cloned.1.call-done = f32[64,128,128]{2,1,0:T(8,128)} async-done(((f32[8,128,128]{2,1,0:T(8,128)}), f32[64,128,128]{2,1,0:T(8,128)}) %all-gather.4.cloned.1.call-update) | async-done | bytes 4194320 | tf_op jit(solution)/shard_map/all_gather | solution.py:11
  139.5 9.7 %while.32 = (s32[]{:T(128)}, f32[8,128,128]{2,1,0:T(8,128)S(1)}, s32[]{:T(128)}, f32[8,8]{1,0:T(8,128)S(1)}, f32[8,8,128,128]{3,2,1,0:T(8,128)}, /*index=5*/s32[]{:T(128)}, s32[]{:T(128)}) while((s32[]{:T(128)}, f32[8,128,128]{2,1,0:T(8,128)S(1)}, s32[]{:T(128)}, f32[8,8]{1,0:T(8,128)S(1)}, f32[8,8,128,128]{3,2,1,0:T(8,128)}, ...), condition=%wide.region_5.6_spmd.clone, body=%wide.region_4.5_spmd.clone.sunk | while | flops 524292 | bytes 1573065 | solution.py:23
  139.5 1.2 fusion.45
  149.3 2.9 %add_convert_fusion = bf16[4,8,128,128]{2,3,1,0:T(8,128)(2,1)} fusion(f32[4,8,128,128]{2,3,1,0:T(8,128)} %get-tuple-element.143, f32[8,128,128]{1,2,0:T(8,128)S(1)} %copy.67, f32[4,8]{1,0:T(4,128)S(1)} %exp.53), kind=kLoop, calls=%fused_computation.21 | loop fusion | flops 1572864 | bytes 3670144 | tf_op jit(solution)/shard_map/convert_element_type | solution.py:62
  152.2 6.1 %all-to-all-start.2 = ((bf16[4,8,128,128]{2,3,1,0:T(8,128)(2,1)}), bf16[4,8,128,128]{2,3,1,0:T(8,128)(2,1)}, u32[]{:S(2)}, u32[]{:S(2)}) async-start(bf16[4,8,128,128]{2,3,1,0:T(8,128)(2,1)} %add_convert_fusion), calls=%async_computation.2 | async-start | bytes 2097152 | tf_op jit(solution)/shard_map/all_to_all | solution.py:61
  158.3 2.0 %select_convert_fusion = bf16[8,256,256]{2,1,0:T(8,128)(2,1)S(1)} fusion(bf16[256,32,128]{0,2,1:T(8,128)(2,1)} %bitcast.143, f32[8,256]{1,0:T(8,128)S(1)} %get-tuple-element.220, pred[256,256]{1,0:T(8,128)(4,1)S(1)} %iota_compare_fusion, bf16[256,32,128]{0,2,1:T(8,128)(2,1)} %bitcast.139), kind=kOutput, calls=%fused_computation.18 | convolution fusion | flops 136839168 | bytes 3751936 | tf_op jit(solution)/shard_map/thd,shd->hts/dot_general | solution.py:73
  160.3 1.5 convolution_bitcast_fusion.4
  161.8 10.0 %all-to-all-done.2 = bf16[4,8,128,128]{2,3,1,0:T(8,128)(2,1)} async-done(((bf16[4,8,128,128]{2,3,1,0:T(8,128)(2,1)}), bf16[4,8,128,128]{2,3,1,0:T(8,128)(2,1)}, u32[]{:S(2)}, u32[]{:S(2)}) %all-to-all-start.2) | async-done | bytes 1048608 | tf_op jit(solution)/shard_map/all_to_all | solution.py:61
  171.9 1.6 fusion.16
  173.7 1.6 fusion.14
  175.4 1.3 fusion.12
  176.7 1.2 fusion.10
  178.4 2.5 %fusion.5 = f32[256,32,128]{0,2,1:T(8,128)} fusion(f32[256,8,128]{0,2,1:T(8,128)S(1)} %fusion.10, f32[256,8,128]{0,2,1:T(8,128)S(1)} %fusion.12, f32[256,8,128]{0,2,1:T(8,128)S(1)} %fusion.14, f32[256,8,128]{0,2,1:T(8,128)S(1)} %fusion.16, f32[256,32]{0,1:T(8,128)S(1)} %add_rsqrt_fusion), kind=kLoop, calls=%fused_computation.16 | loop fusion | flops 4194304 | bytes 8421376 | tf_op jit(solution)/shard_map/mul | solution.py:86
  180.9 5.7 %copy.75 = f32[256,4096]{1,0:T(8,128)} copy(f32[256,4096]{0,1:T(8,128)} %bitcast.136) | data formatting | bytes 8388608 | tf_op jit(solution)/shard_map/mul | solution.py:86
  186.6 3.9 %multiply_convert_fusion = bf16[256,4096]{1,0:T(8,128)(2,1)} fusion(f32[256,4096]{1,0:T(8,128)} %copy.75, f32[4096]{0:T(1024)S(1)} %copy-done.7), kind=kLoop, calls=%fused_computation.13 | loop fusion | flops 2097152 | bytes 6307840 | tf_op jit(solution)/shard_map/convert_element_type | solution.py:87
  (80 shorter events, 19.4 us)
Async XLA Ops:
  6.5 0.8 copy-start
  9.0 15.3 %all-to-all-start = ((f32[1,4,8]{2,0,1:T(1,128)}), f32[1,4,8]{2,0,1:T(1,128)S(1)}, u32[]{:S(2)}, u32[]{:S(2)}) async-start(f32[1,4,8]{2,0,1:T(1,128)} %bitcast.5), calls=%async_computation | async-start | bytes 4096 | tf_op jit(solution)/shard_map/all_to_all | solution.py:54
  24.4 29.2 %all-to-all-start.1 = ((f32[1,32,128,128]{3,2,0,1:T(8,128)}), f32[1,32,128,128]{3,2,0,1:T(8,128)}, u32[]{:S(2)}, u32[]{:S(2)}) async-start(f32[1,32,128,128]{3,2,0,1:T(8,128)} %fusion.8), calls=%async_computation.1 | async-start | bytes 4194304 | tf_op jit(solution)/shard_map/all_to_all | solution.py:53
  28.8 110.7 %all-gather.4.cloned.1.call-start = ((), (), s32[]{:S(2)}) async-start(), calls=%async_computation.3 | async-start | bytes 4718592 | tf_op jit(solution)/shard_map/all_gather | solution.py:11
  66.3 4.1 %copy-start.8 = (u32[32]{0:T(128)S(1)}, u32[32]{0:T(128)}, u32[]{:S(2)}) copy-start(u32[32]{0:T(128)} %constant.60) | copy-start | bytes 388
  71.7 3.6 %copy-start.2 = (bf16[256,4096]{0,1:T(8,128)(2,1)S(1)}, bf16[256,4096]{0,1:T(8,128)(2,1)}, u32[]{:S(2)}) copy-start(bf16[256,4096]{0,1:T(8,128)(2,1)} %copy.57) | copy-start | bytes 6291460
  73.8 2.0 %copy-start.1 = (bf16[256,4096]{0,1:T(8,128)(2,1)S(1)}, bf16[256,4096]{0,1:T(8,128)(2,1)}, u32[]{:S(2)}) copy-start(bf16[256,4096]{0,1:T(8,128)(2,1)} %copy.59) | copy-start | bytes 6291460
  152.2 19.7 %all-to-all-start.2 = ((bf16[4,8,128,128]{2,3,1,0:T(8,128)(2,1)}), bf16[4,8,128,128]{2,3,1,0:T(8,128)(2,1)}, u32[]{:S(2)}, u32[]{:S(2)}) async-start(bf16[4,8,128,128]{2,3,1,0:T(8,128)(2,1)} %add_convert_fusion), calls=%async_computation.2 | async-start | bytes 2097152 | tf_op jit(solution)/shard_map/all_to_all | solution.py:61
  160.3 11.6 %copy-start.4 = (f32[256,8,128]{0,2,1:T(8,128)S(1)}, f32[256,8,128]{0,2,1:T(8,128)}, u32[]{:S(2)}) copy-start(f32[256,8,128]{0,2,1:T(8,128)} %convolution_bitcast_fusion.7) | copy-start | bytes 3145732
  171.9 1.8 copy-start.3
  173.4 1.9 copy-start.5
  175.3 1.3 copy-start.6
  180.9 5.7 %copy-start.7 = (f32[4096]{0:T(1024)S(1)}, f32[4096]{0:T(1024)}, u32[]{:S(2)}) copy-start(f32[4096]{0:T(1024)} %param.13) | copy-start | bytes 49156
Sparse Core Ops, SparseCore 0:
  66.4 72.9 all-gather.3
where the time goes:
time: 200 us; the launch traced here: 197 us
  waiting for transfers between devices  74.5 us (37%)
  other arithmetic  28.3 us (14%)
  local copies, waits for them, and re-layouts  25.2 us (13%)
  matrix products  21.1 us (11%)
  blocking collectives  18.9 us (9%)
  starting transfers between devices  14.8 us (7%)
  between operations  14.2 us (7%)
    all_gather x1, waiting for transfers between devices, entering(): everything = jax.tree.map(lambda part: lax.all_gather(part, axis), shard)  39.8 us
    all_to_all x1, waiting for transfers between devices, on_device(): lax.all_to_all(block_state[None], 'narrow', split_axis=1, concat_axis=0,...  24.7 us
    unnamed x1, blocking collectives  18.9 us
    unnamed x24, local copies, waits for them, and re-layouts  13.8 us
    all_to_all x1, waiting for transfers between devices, on_device(): lax.all_to_all(prefix.astype(jnp.bfloat16), 'narrow', split_axis=0, conca...  10 us
    select_n x8, other arithmetic, hop(): return jax.tree.map(lambda a, b: jnp.where(reached, a, b), new, before)  9.38 us
    broadcast_in_dim x6, other arithmetic, group_prefix(): whole, before = lax.scan(advance, start, (totals, states))  8.26 us
    all_to_all x1, starting transfers between devices, on_device(): lax.all_to_all(prefix.astype(jnp.bfloat16), 'narrow', split_axis=0, conca...  6.08 us
  transfers between devices with their start and end apart: 4, of which 3 were waited for; matrix products, arithmetic and copies ran while one was open for 14% of the time, Pallas kernels for 0%

commit v1 on v0

v1 whole, which is shorter than its diff:
```python
import functools

import jax
import jax.numpy as jnp
from jax import lax
from jax.experimental import pallas as pl
from jax.experimental.pallas import tpu as pltpu
from jax.sharding import PartitionSpec as P

MESH = pl.DeviceIdType.MESH
FAR = -1e30


def split_outer(outer):
    rows = 1
    for d in range(1, outer + 1):
        if d * d <= outer and outer % d == 0:
            rows = d
    return outer // rows, rows


def kernel(
    sizes, q_ref, k_ref, v_ref, ld_ref, gain_ref, out_ref,
    cum, decay_cols, tail_cols, head_cols, bias, inner,
    made, got1, t1, wsend, got2, t2, got3, t3, gsend, got4, csend, carried,
    send_sem, recv_sem, tsend_sem, trecv_sem,
):
    narrow, depth, rows, heads, width, unit = sizes
    tokens = q_ref.shape[0]
    own = heads // narrow
    sub = own // rows
    o, n = lax.axis_index("outer"), lax.axis_index("narrow")
    z, y = o // rows, lax.rem(o, rows)

    order = [narrow // 2 + i for i in range(narrow)]
    near = [lax.rem(n + i % narrow, narrow) for i in order if i % narrow]
    level = [lax.rem(y + i, rows) for i in range(1, rows)]
    deep = [lax.rem(z + i, depth) for i in range(1, depth)]

    barrier = pltpu.get_barrier_semaphore()
    peers = [(o, j) for j in near]
    peers += [(z * rows + j, n) for j in level]
    peers += [(j * rows + y, n) for j in deep]
    for peer in peers:
        pl.semaphore_signal(barrier, inc=1, device_id=peer, device_id_type=MESH)

    def copy(src, dst, ssem, rsem, peer):
        return pltpu.make_async_remote_copy(
            src_ref=src, dst_ref=dst, send_sem=ssem, recv_sem=rsem,
            device_id=peer, device_id_type=MESH,
        )

    total = ld_ref[...]
    lane = lax.broadcasted_iota(jnp.int32, total.shape, 1)
    step = 1
    while step < tokens:
        total = total + jnp.where(lane >= step, pltpu.roll(total, step, axis=1), 0.0)
        step *= 2
    cum[...] = total
    t1[n] = jnp.broadcast_to(total[:, tokens - 1 :], (heads, width))
    cols = jnp.concatenate([total, jnp.zeros((128 - heads, tokens), jnp.float32)], axis=0).T
    tail = jnp.exp(cols[tokens - 1 :] - cols)
    grown = jnp.exp(cols)
    for g in range(heads // unit):
        shift = (128 - g * unit) % 128
        for ref, value in ((decay_cols, cols), (tail_cols, tail), (head_cols, grown)):
            ref[g] = pltpu.roll(value, shift, axis=1) if shift else value
    at_t = lax.broadcasted_iota(jnp.int32, (tokens, tokens), 0)
    at_s = lax.broadcasted_iota(jnp.int32, (tokens, tokens), 1)
    bias[...] = jnp.where(at_t >= at_s, 0.0, FAR)

    def lanes(h):
        return pl.ds(pl.multiple_of(h * width, width), width)

    def states(j):
        def body(i, _):
            g = j * (own // unit) + i
            tails = tail_cols[g]
            for u in range(unit):
                at = lanes(g * unit + u)
                kept = k_ref[:, at].astype(jnp.float32) * tails[:, u : u + 1]
                made[j, i * unit + u] = lax.dot_general(
                    kept.astype(jnp.bfloat16), v_ref[:, at], (((0,), (0,)), ((), ())),
                    preferred_element_type=jnp.float32,
                ).astype(jnp.bfloat16)
            return 0

        lax.fori_loop(0, own // unit, body, 0)

    def within(first, last):
        def body(g, _):
            columns = decay_cols[g]
            for u in range(unit):
                h = g * unit + u
                at = lanes(h)
                scores = lax.dot_general(
                    q_ref[:, at], k_ref[:, at], (((1,), (1,)), ((), ())),
                    preferred_element_type=jnp.float32,
                )
                spread = columns[:, u : u + 1] - cum[pl.ds(h, 1), :] + bias[...]
                weights = (scores * jnp.exp(spread)).astype(jnp.bfloat16)
                inner[:, at] = jnp.dot(weights, v_ref[:, at], preferred_element_type=jnp.float32)
            return 0

        lax.fori_loop(first, last, body, 0)

    def finish(j):
        def body(i, _):
            g = j * (own // unit) + i
            grow = head_cols[g]
            for u in range(unit):
                at = lanes(g * unit + u)
                read = jnp.dot(
                    q_ref[:, at], carried[j, i * unit + u], preferred_element_type=jnp.float32
                )
                numer = inner[:, at] + read * grow[:, u : u + 1]
                mean = jnp.mean(numer * numer, axis=-1, keepdims=True)
                out_ref[:, at] = (numer * lax.rsqrt(mean + 1e-06) * gain_ref[:, at]).astype(
                    jnp.bfloat16
                )
            return 0

        lax.fori_loop(0, own // unit, body, 0)

    groups = heads // unit
    marks = [groups * c // 32 for c in (0, 12, 16, 28, 32)]

    pl.semaphore_wait(barrier, len(peers))
    pending = []

    def begin(one):
        one.start()
        pending.append(one)

    for i, j in enumerate(near):
        begin(copy(t1.at[n], t1.at[n], tsend_sem.at[0, i], trecv_sem.at[0, n], (o, j)))
    for i, j in enumerate(near):
        states(j)
        begin(copy(made.at[j], got1.at[n], send_sem.at[0, i], recv_sem.at[0, n], (o, j)))
    states(n)
    got1[n] = made[n]
    for i, j in enumerate(near):
        copy(t1.at[j], t1.at[j], tsend_sem.at[0, i], trecv_sem.at[0, j], (o, j)).wait_recv()
    group_total = t1[0]
    for j in range(1, narrow):
        group_total = group_total + t1[j]
    t2[y] = group_total
    for i, j in enumerate(level):
        begin(copy(t2.at[y], t2.at[y], tsend_sem.at[1, i], trecv_sem.at[1, y], (z * rows + j, n)))
    within(marks[0], marks[1])
    for i, j in enumerate(near):
        copy(made.at[j], got1.at[j], send_sem.at[0, i], recv_sem.at[0, j], (o, j)).wait_recv()

    def decay(ref, j, k):
        return jnp.exp(ref[j, pl.ds(n * own + k, 1), :])

    def sum_group(k, _):
        acc = got1[0, k].astype(jnp.float32)
        for j in range(1, narrow):
            acc = decay(t1, j, k) * acc + got1[j, k].astype(jnp.float32)
        wsend[k] = acc.astype(jnp.bfloat16)
        return 0

    lax.fori_loop(0, own, sum_group, 0)
    for i, j in enumerate(level):
        begin(
            copy(
                wsend.at[pl.ds(j * sub, sub)], got2.at[y], send_sem.at[1, i], recv_sem.at[1, y],
                (z * rows + j, n),
            )
        )
    got2[y] = wsend[pl.ds(y * sub, sub)]
    for i, j in enumerate(level):
        copy(t2.at[j], t2.at[j], tsend_sem.at[1, i], trecv_sem.at[1, j], (z * rows + j, n)).wait_recv()
    row_total = t2[0]
    for j in range(1, rows):
        row_total = row_total + t2[j]
    t3[z] = row_total
    for i, j in enumerate(deep):
        begin(copy(t3.at[z], t3.at[z], tsend_sem.at[2, i], trecv_sem.at[2, z], (j * rows + y, n)))
    within(marks[1], marks[2])
    for i, j in enumerate(level):
        copy(
            wsend.at[pl.ds(j * sub, sub)], got2.at[j], send_sem.at[1, i], recv_sem.at[1, j],
            (z * rows + j, n),
        ).wait_recv()

    def sum_row(k, _):
        acc = got2[0, k].astype(jnp.float32)
        for j in range(1, rows):
            acc = decay(t2, j, y * sub + k) * acc + got2[j, k].astype(jnp.float32)
        got3[z, k] = acc.astype(jnp.bfloat16)
        return 0

    lax.fori_loop(0, sub, sum_row, 0)
    for i, j in enumerate(deep):
        begin(copy(got3.at[z], got3.at[z], send_sem.at[2, i], recv_sem.at[2, z], (j * rows + y, n)))
    within(marks[2], marks[3])
    for i, j in enumerate(deep):
        copy(t3.at[j], t3.at[j], tsend_sem.at[2, i], trecv_sem.at[2, j], (j * rows + y, n)).wait_recv()
        copy(got3.at[j], got3.at[j], send_sem.at[2, i], recv_sem.at[2, j], (j * rows + y, n)).wait_recv()

    def enter_row(k, _):
        at = y * sub + k
        acc = jnp.zeros((width, width), jnp.float32)
        for j in range(depth - 1):
            new = decay(t3, j, at) * acc + got3[j, k].astype(jnp.float32)
            acc = jnp.where(j < z, new, acc)
        for j in range(rows):
            gsend[j, k] = acc.astype(jnp.bfloat16)
            acc = decay(t2, j, at) * acc + got2[j, k].astype(jnp.float32)
        return 0

    lax.fori_loop(0, sub, enter_row, 0)
    for i, j in enumerate(level):
        begin(copy(gsend.at[j], got4.at[y], send_sem.at[3, i], recv_sem.at[3, y], (z * rows + j, n)))
    got4[y] = gsend[y]
    within(marks[3], marks[4])
    for i, j in enumerate(level):
        copy(gsend.at[j], got4.at[j], send_sem.at[3, i], recv_sem.at[3, j], (z * rows + j, n)).wait_recv()

    def enter_group(k, _):
        acc = got4[k // sub, lax.rem(k, sub)].astype(jnp.float32)
        for j in range(narrow):
            csend[j, k] = acc.astype(jnp.bfloat16)
            acc = decay(t1, j, k) * acc + got1[j, k].astype(jnp.float32)
        return 0

    lax.fori_loop(0, own, enter_group, 0)
    for i, j in enumerate(near):
        begin(copy(csend.at[j], carried.at[n], send_sem.at[4, i], recv_sem.at[4, n], (o, j)))
    carried[n] = csend[n]
    finish(n)
    for i, j in enumerate(near[::-1]):
        copy(csend.at[j], carried.at[j], send_sem.at[4, i], recv_sem.at[4, j], (o, j)).wait_recv()
        finish(j)
    for one in pending:
        one.wait_send()


def on_device(mesh_sizes, queries, keys, values, log_decay, gain):
    outer, narrow = mesh_sizes
    tokens, model = queries.shape
    heads = log_decay.shape[0]
    width = model // heads
    depth, rows = split_outer(outer)
    own = heads // narrow
    sub = own // rows
    unit = min(4, own)
    half = lambda *shape: pltpu.VMEM(shape + (width, width), jnp.bfloat16)
    full = lambda *shape: pltpu.VMEM(shape, jnp.float32)
    most = max(narrow, depth, rows)
    dma = lambda *shape: pltpu.SemaphoreType.DMA(shape)
    vmem = pl.BlockSpec(memory_space=pltpu.VMEM)
    return pl.pallas_call(
        functools.partial(kernel, (narrow, depth, rows, heads, width, unit)),
        out_shape=jax.ShapeDtypeStruct(queries.shape, jnp.bfloat16),
        in_specs=[vmem] * 5,
        out_specs=vmem,
        scratch_shapes=[
            full(heads, tokens),
            full(heads // unit, tokens, 128),
            full(heads // unit, tokens, 128),
            full(heads // unit, tokens, 128),
            full(tokens, tokens),
            full(tokens, model),
            half(narrow, own),
            half(narrow, own),
            full(narrow, heads, width),
            half(own),
            half(rows, sub),
            full(rows, heads, width),
            half(depth, sub),
            full(depth, heads, width),
            half(rows, sub),
            half(rows, sub),
            half(narrow, own),
            half(narrow, own),
            dma(5, most),
            dma(5, most),
            dma(3, most),
            dma(3, most),
        ],
        compiler_params=pltpu.CompilerParams(
            collective_id=0, has_side_effects=True, vmem_limit_bytes=48 * 1024 * 1024
        ),
    )(queries, keys, values, log_decay, gain.reshape(1, model))


def solution(mesh):
    axes = ("outer", "narrow")
    block = P(axes, None)
    return jax.shard_map(
        functools.partial(on_device, tuple(mesh.shape[a] for a in axes)),
        mesh=mesh,
        in_specs=(block, block, block, P(None, axes), P()),
        out_specs=block,
        check_vma=False,
    )
```

time: 200 us -> 61.5 us (0.31)
  the two profiles are of different devices: /device:TPU:1 before, /device:TPU:11 now
where the time goes in v1:
time: 61.5 us; the launch traced here: 61.2 us
  Pallas kernels  56.8 us (92%)
  local copies, waits for them, and re-layouts  4.39 us (7%)
    pallas_call x1, Pallas kernels, on_device(): pl.pallas_call(functools.partial(kernel, (narrow, depth, rows, heads, wid...  56.8 us
    unnamed x7, local copies, waits for them, and re-layouts  4.39 us

profile of v1, /device:TPU:11, one launch (start us, length us, event | category | flops | bytes accessed | tf_op | source)
XLA Modules:
  0.0 61.2 jit_solution(3848108923653850141)
XLA Ops:
  0.0 0.0 copy-start
  0.0 1.6 %copy-done = bf16[256,4096]{1,0:T(8,128)(2,1)S(1)} copy-done((bf16[256,4096]{1,0:T(8,128)(2,1)S(1)}, bf16[256,4096]{1,0:T(8,128)(2,1)}, u32[]{:S(2)}) %copy-start) | copy-done | bytes 2097176
  1.6 0.0 copy-start.1
  1.6 0.8 %copy-done.1 = f32[32,256]{1,0:T(8,128)S(1)} copy-done((f32[32,256]{1,0:T(8,128)S(1)}, f32[32,256]{1,0:T(8,128)}, u32[]{:S(2)}) %copy-start.1) | copy-done | bytes 32792
  2.4 0.0 copy-start.2
  2.4 0.7 %copy-done.2 = f32[4096]{0:T(1024)S(1)} copy-done((f32[4096]{0:T(1024)S(1)}, f32[4096]{0:T(1024)}, u32[]{:S(2)}) %copy-start.2) | copy-done | bytes 16408
  3.1 56.8 %shard_map.55 = bf16[256,4096]{1,0:T(8,128)(2,1)S(1)} custom-call(bf16[256,4096]{1,0:T(8,128)(2,1)S(1)} %copy-done, bf16[256,4096]{1,0:T(8,128)(2,1)} %k_ref.1, bf16[256,4096]{1,0:T(8,128)(2,1)} %v_ref.1, f32[32,256]{1,0:T(8,128)S(1)} %copy-done.1, f32[1,4096]{1,0:T(1,128)S(1)} %bitcast.1), custom_call_target="tpu_custom_call" | custom-call | tf_op jit(solution)/shard_map/pallas_call | solution.py:255
  59.9 1.3 %copy.7 = bf16[256,4096]{1,0:T(8,128)(2,1)} copy(bf16[256,4096]{1,0:T(8,128)(2,1)S(1)} %shard_map.55) | data formatting | bytes 4194304
Async XLA Ops:
  0.0 1.6 %copy-start = (bf16[256,4096]{1,0:T(8,128)(2,1)S(1)}, bf16[256,4096]{1,0:T(8,128)(2,1)}, u32[]{:S(2)}) copy-start(bf16[256,4096]{1,0:T(8,128)(2,1)} %q_ref.1) | copy-start | bytes 6291460
  1.6 0.8 %copy-start.1 = (f32[32,256]{1,0:T(8,128)S(1)}, f32[32,256]{1,0:T(8,128)}, u32[]{:S(2)}) copy-start(f32[32,256]{1,0:T(8,128)} %ld_ref.1) | copy-start | bytes 98308
  2.4 0.7 %copy-start.2 = (f32[4096]{0:T(1024)S(1)}, f32[4096]{0:T(1024)}, u32[]{:S(2)}) copy-start(f32[4096]{0:T(1024)} %param.9) | copy-start | bytes 49156

commit v2 on v1

v2 whole, which is shorter than its diff:
```python
import functools

import jax
import jax.numpy as jnp
from jax import lax
from jax.experimental import pallas as pl
from jax.experimental.pallas import tpu as pltpu
from jax.sharding import PartitionSpec as P

MESH = pl.DeviceIdType.MESH
FAR = -1e30


def split_outer(outer):
    rows = 1
    for d in range(1, outer + 1):
        if d * d <= outer and outer % d == 0:
            rows = d
    return outer // rows, rows


def kernel(
    sizes, q_hbm, k_hbm, v_hbm, ld_ref, gain_ref, out_ref,
    q_ref, k_ref, v_ref, cum, decay_cols, tail_cols, head_cols, bias, inner,
    made, got1, t1, wsend, got2, t2, got3, t3, gsend, got4, csend, carried,
    load_sem, send_sem, recv_sem, tsend_sem, trecv_sem,
):
    narrow, depth, rows, heads, width, unit = sizes
    tokens = q_ref.shape[0]
    own = heads // narrow
    chunks = own // rows
    o, n = lax.axis_index("outer"), lax.axis_index("narrow")
    z, y = o // rows, lax.rem(o, rows)

    near = [lax.rem(n + i % narrow, narrow) for i in range(narrow // 2, narrow // 2 + narrow) if i % narrow]
    level = [lax.rem(y + i, rows) for i in range(1, rows)]
    deep = [lax.rem(z + i, depth) for i in range(1, depth)]
    group_at = lambda j: (o, j)
    row_at = lambda j: (z * rows + j, n)
    depth_at = lambda j: (j * rows + y, n)

    loads = [
        pltpu.make_async_copy(src, dst, load_sem.at[i])
        for i, (src, dst) in enumerate(((k_hbm, k_ref), (v_hbm, v_ref), (q_hbm, q_ref)))
    ]
    for one in loads:
        one.start()

    barrier = pltpu.get_barrier_semaphore()
    peers = [group_at(j) for j in near] + [row_at(j) for j in level] + [depth_at(j) for j in deep]
    for peer in peers:
        pl.semaphore_signal(barrier, inc=1, device_id=peer, device_id_type=MESH)

    total = ld_ref[...]
    lane = lax.broadcasted_iota(jnp.int32, total.shape, 1)
    step = 1
    while step < tokens:
        total = total + jnp.where(lane >= step, pltpu.roll(total, step, axis=1), 0.0)
        step *= 2
    cum[...] = total
    t1[n] = jnp.broadcast_to(total[:, tokens - 1 :], (heads, width))
    cols = jnp.concatenate([total, jnp.zeros((128 - heads, tokens), jnp.float32)], axis=0).T
    tail = jnp.exp(cols[tokens - 1 :] - cols)
    grown = jnp.exp(cols)
    for g in range(heads // unit):
        shift = (128 - g * unit) % 128
        for ref, value in ((decay_cols, cols), (tail_cols, tail), (head_cols, grown)):
            ref[g] = pltpu.roll(value, shift, axis=1) if shift else value
    at_t = lax.broadcasted_iota(jnp.int32, (tokens, tokens), 0)
    at_s = lax.broadcasted_iota(jnp.int32, (tokens, tokens), 1)
    bias[...] = jnp.where(at_t >= at_s, 0.0, FAR)

    def lanes(h):
        return pl.ds(pl.multiple_of(h * width, width), width)

    def states(c):
        def body(j, _):
            for r in range(rows):
                k = c * rows + r
                at = lanes(j * own + k)
                tails = tail_cols[j * (own // unit) + k // unit]
                u = k % unit
                kept = k_ref[:, at].astype(jnp.float32) * tails[:, u : u + 1]
                made[c, j, r] = lax.dot_general(
                    kept.astype(jnp.bfloat16), v_ref[:, at], (((0,), (0,)), ((), ())),
                    preferred_element_type=jnp.float32,
                ).astype(jnp.bfloat16)
            return 0

        lax.fori_loop(0, narrow, body, 0, unroll=2)

    def within(first, last):
        def body(g, _):
            columns = decay_cols[g]
            for u in range(unit):
                h = g * unit + u
                at = lanes(h)
                scores = lax.dot_general(
                    q_ref[:, at], k_ref[:, at], (((1,), (1,)), ((), ())),
                    preferred_element_type=jnp.float32,
                )
                spread = columns[:, u : u + 1] - cum[pl.ds(h, 1), :] + bias[...]
                weights = (scores * jnp.exp(spread)).astype(jnp.bfloat16)
                inner[:, at] = jnp.dot(weights, v_ref[:, at], preferred_element_type=jnp.float32)
            return 0

        lax.fori_loop(first, last, body, 0)

    def finish(c, j):
        for r in range(rows):
            k = c * rows + r
            at = lanes(j * own + k)
            grow = head_cols[j * (own // unit) + k // unit]
            u = k % unit
            read = jnp.dot(q_ref[:, at], carried[c, j, r], preferred_element_type=jnp.float32)
            numer = inner[:, at] + read * grow[:, u : u + 1]
            mean = jnp.mean(numer * numer, axis=-1, keepdims=True)
            out_ref[:, at] = (numer * lax.rsqrt(mean + 1e-06) * gain_ref[:, at]).astype(jnp.bfloat16)

    pending = []

    def begin(kind, c, src, dst, peers_of, where, mine):
        for i, j in enumerate(peers_of):
            one = pltpu.make_async_remote_copy(
                src_ref=src(j), dst_ref=dst(mine), send_sem=send_sem.at[kind, c, i],
                recv_sem=recv_sem.at[kind, c, mine], device_id=where(j), device_id_type=MESH,
            )
            one.start()
            pending.append(one)

    def arrive(kind, c, dst, peers_of, where):
        for i, j in enumerate(peers_of):
            pltpu.make_async_remote_copy(
                src_ref=dst(j), dst_ref=dst(j), send_sem=send_sem.at[kind, c, i],
                recv_sem=recv_sem.at[kind, c, j], device_id=where(j), device_id_type=MESH,
            ).wait_recv()

    def begin_total(kind, ref, mine, peers_of, where):
        for i, j in enumerate(peers_of):
            one = pltpu.make_async_remote_copy(
                src_ref=ref.at[mine], dst_ref=ref.at[mine], send_sem=tsend_sem.at[kind, i],
                recv_sem=trecv_sem.at[kind, mine], device_id=where(j), device_id_type=MESH,
            )
            one.start()
            pending.append(one)

    def arrive_total(kind, ref, peers_of, where):
        for i, j in enumerate(peers_of):
            pltpu.make_async_remote_copy(
                src_ref=ref.at[j], dst_ref=ref.at[j], send_sem=tsend_sem.at[kind, i],
                recv_sem=trecv_sem.at[kind, j], device_id=where(j), device_id_type=MESH,
            ).wait_recv()

    def decay(ref, j, k):
        return jnp.exp(ref[j, pl.ds(n * own + k, 1), :])

    def stage0(c):
        states(c)
        begin(0, c, lambda j: made.at[c, j], lambda j: got1.at[c, j], near, group_at, n)
        got1[c, n] = made[c, n]

    def stage1(c):
        arrive(0, c, lambda j: got1.at[c, j], near, group_at)
        for r in range(rows):
            acc = got1[c, 0, r].astype(jnp.float32)
            for j in range(1, narrow):
                acc = decay(t1, j, c * rows + r) * acc + got1[c, j, r].astype(jnp.float32)
            wsend[c, r] = acc.astype(jnp.bfloat16)
        begin(1, c, lambda j: wsend.at[c, j], lambda j: got2.at[c, j], level, row_at, y)
        got2[c, y] = wsend[c, y]

    def stage2(c):
        arrive(1, c, lambda j: got2.at[c, j], level, row_at)
        acc = got2[c, 0].astype(jnp.float32)
        for j in range(1, rows):
            acc = decay(t2, j, c * rows + y) * acc + got2[c, j].astype(jnp.float32)
        got3[c, z] = acc.astype(jnp.bfloat16)
        begin(2, c, lambda j: got3.at[c, z], lambda j: got3.at[c, j], deep, depth_at, z)

    def stage3(c):
        arrive(2, c, lambda j: got3.at[c, j], deep, depth_at)
        k = c * rows + y
        acc = jnp.zeros((width, width), jnp.float32)
        for j in range(depth - 1):
            new = decay(t3, j, k) * acc + got3[c, j].astype(jnp.float32)
            acc = jnp.where(j < z, new, acc)
        for j in range(rows):
            gsend[c, j] = acc.astype(jnp.bfloat16)
            if j < rows - 1:
                acc = decay(t2, j, k) * acc + got2[c, j].astype(jnp.float32)
        begin(3, c, lambda j: gsend.at[c, j], lambda j: got4.at[c, j], level, row_at, y)
        got4[c, y] = gsend[c, y]

    def stage4(c):
        arrive(3, c, lambda j: got4.at[c, j], level, row_at)
        for r in range(rows):
            acc = got4[c, r].astype(jnp.float32)
            for j in range(narrow):
                csend[c, j, r] = acc.astype(jnp.bfloat16)
                if j < narrow - 1:
                    acc = decay(t1, j, c * rows + r) * acc + got1[c, j, r].astype(jnp.float32)
        begin(4, c, lambda j: csend.at[c, j], lambda j: carried.at[c, j], near, group_at, n)
        carried[c, n] = csend[c, n]

    def stage5(c):
        arrive(4, c, lambda j: carried.at[c, j], near, group_at)

        def body(j, _):
            finish(c, j)
            return 0

        lax.fori_loop(0, narrow, body, 0, unroll=2)

    def totals1():
        arrive_total(0, t1, near, group_at)
        group_total = t1[0]
        for j in range(1, narrow):
            group_total = group_total + t1[j]
        t2[y] = group_total
        begin_total(1, t2, y, level, row_at)

    def totals2():
        arrive_total(1, t2, level, row_at)
        row_total = t2[0]
        for j in range(1, rows):
            row_total = row_total + t2[j]
        t3[z] = row_total
        begin_total(2, t3, z, deep, depth_at)

    pl.semaphore_wait(barrier, len(peers))
    begin_total(0, t1, n, near, group_at)
    loads[0].wait()
    loads[1].wait()
    for c in range(chunks):
        stage0(c)
    totals1()
    loads[2].wait()

    groups = heads // unit
    events = [(TIMES[p] + GAP * c, p, c) for p in range(5) for c in range(chunks)]
    events += [(TIMES[1] - 0.1, 5, 0), (TIMES[2] - 0.1, 6, 0)]
    early = min(groups, EARLY)
    within(0, early)
    filled = early
    for _, p, c in sorted(events):
        if p == 4 and filled < groups:
            within(filled, groups)
            filled = groups
        if p == 5:
            totals2()
        elif p == 6:
            arrive_total(2, t3, deep, depth_at)
        else:
            (stage1, stage2, stage3, stage4, stage5)[p](c)
            if filled < groups:
                within(filled, filled + 1)
                filled += 1
    for one in pending:
        one.wait_send()


TIMES = (5.4, 7.8, 12.8, 15.2, 19.6)
GAP = 2.75
EARLY = 2


def on_device(mesh_sizes, queries, keys, values, log_decay, gain):
    outer, narrow = mesh_sizes
    tokens, model = queries.shape
    heads = log_decay.shape[0]
    width = model // heads
    depth, rows = split_outer(outer)
    own = heads // narrow
    chunks = own // rows
    unit = min(4, own)
    half = lambda *shape: pltpu.VMEM(shape + (width, width), jnp.bfloat16)
    full = lambda *shape: pltpu.VMEM(shape, jnp.float32)
    most = max(narrow, depth, rows)
    dma = lambda *shape: pltpu.SemaphoreType.DMA(shape)
    vmem = pl.BlockSpec(memory_space=pltpu.VMEM)
    hbm = pl.BlockSpec(memory_space=pltpu.HBM)
    return pl.pallas_call(
        functools.partial(kernel, (narrow, depth, rows, heads, width, unit)),
        out_shape=jax.ShapeDtypeStruct(queries.shape, jnp.bfloat16),
        in_specs=[hbm] * 3 + [vmem] * 2,
        out_specs=vmem,
        scratch_shapes=[
            pltpu.VMEM((tokens, model), queries.dtype),
            pltpu.VMEM((tokens, model), queries.dtype),
            pltpu.VMEM((tokens, model), queries.dtype),
            full(heads, tokens),
            full(heads // unit, tokens, 128),
            full(heads // unit, tokens, 128),
            full(heads // unit, tokens, 128),
            full(tokens, tokens),
            full(tokens, model),
            half(chunks, narrow, rows),
            half(chunks, narrow, rows),
            full(narrow, heads, width),
            half(chunks, rows),
            half(chunks, rows),
            full(rows, heads, width),
            half(chunks, depth),
            full(depth, heads, width),
            half(chunks, rows),
            half(chunks, rows),
            half(chunks, narrow, rows),
            half(chunks, narrow, rows),
            dma(3),
            dma(5, chunks, most),
            dma(5, chunks, most),
            dma(3, most),
            dma(3, most),
        ],
        compiler_params=pltpu.CompilerParams(
            collective_id=0, has_side_effects=True, vmem_limit_bytes=48 * 1024 * 1024
        ),
    )(queries, keys, values, log_decay, gain.reshape(1, model))


def solution(mesh):
    axes = ("outer", "narrow")
    block = P(axes, None)
    return jax.shard_map(
        functools.partial(on_device, tuple(mesh.shape[a] for a in axes)),
        mesh=mesh,
        in_specs=(block, block, block, P(None, axes), P()),
        out_specs=block,
        check_vma=False,
    )
```

time: 61.5 us -> 43.1 us (0.70)
  the two profiles are of different devices: /device:TPU:11 before, /device:TPU:1 now
where the time goes in v2:
time: 43.1 us; the launch traced here: 42.8 us
  Pallas kernels  38.4 us (89%)
  local copies, waits for them, and re-layouts  4.39 us (10%)
    pallas_call x1, Pallas kernels, on_device(): pl.pallas_call(functools.partial(kernel, (narrow, depth, rows, heads, wid...  38.4 us
    unnamed x7, local copies, waits for them, and re-layouts  4.39 us

profile of v2, /device:TPU:1, one launch (start us, length us, event | category | flops | bytes accessed | tf_op | source)
XLA Modules:
  0.0 42.8 jit_solution(12882221686801072213)
XLA Ops:
  0.0 0.0 copy-start
  0.0 1.6 %copy-done = bf16[256,4096]{1,0:T(8,128)(2,1)S(1)} copy-done((bf16[256,4096]{1,0:T(8,128)(2,1)S(1)}, bf16[256,4096]{1,0:T(8,128)(2,1)}, u32[]{:S(2)}) %copy-start) | copy-done | bytes 2097176
  1.6 0.0 copy-start.1
  1.6 0.8 %copy-done.1 = f32[32,256]{1,0:T(8,128)S(1)} copy-done((f32[32,256]{1,0:T(8,128)S(1)}, f32[32,256]{1,0:T(8,128)}, u32[]{:S(2)}) %copy-start.1) | copy-done | bytes 32792
  2.4 0.0 copy-start.2
  2.4 0.7 %copy-done.2 = f32[4096]{0:T(1024)S(1)} copy-done((f32[4096]{0:T(1024)S(1)}, f32[4096]{0:T(1024)}, u32[]{:S(2)}) %copy-start.2) | copy-done | bytes 16408
  3.1 38.4 %shard_map.55 = bf16[256,4096]{1,0:T(8,128)(2,1)S(1)} custom-call(bf16[256,4096]{1,0:T(8,128)(2,1)S(1)} %copy-done, bf16[256,4096]{1,0:T(8,128)(2,1)} %k_hbm.1, bf16[256,4096]{1,0:T(8,128)(2,1)} %v_hbm.1, f32[32,256]{1,0:T(8,128)S(1)} %copy-done.1, f32[1,4096]{1,0:T(1,128)S(1)} %bitcast.1), custom_call_target="tpu_custom_call" | custom-call | tf_op jit(solution)/shard_map/pallas_call | solution.py:282
  41.5 1.3 %copy.7 = bf16[256,4096]{1,0:T(8,128)(2,1)} copy(bf16[256,4096]{1,0:T(8,128)(2,1)S(1)} %shard_map.55) | data formatting | bytes 4194304
Async XLA Ops:
  0.0 1.6 %copy-start = (bf16[256,4096]{1,0:T(8,128)(2,1)S(1)}, bf16[256,4096]{1,0:T(8,128)(2,1)}, u32[]{:S(2)}) copy-start(bf16[256,4096]{1,0:T(8,128)(2,1)} %q_hbm.1) | copy-start | bytes 6291460
  1.6 0.8 %copy-start.1 = (f32[32,256]{1,0:T(8,128)S(1)}, f32[32,256]{1,0:T(8,128)}, u32[]{:S(2)}) copy-start(f32[32,256]{1,0:T(8,128)} %ld_ref.1) | copy-start | bytes 98308
  2.4 0.7 %copy-start.2 = (f32[4096]{0:T(1024)S(1)}, f32[4096]{0:T(1024)}, u32[]{:S(2)}) copy-start(f32[4096]{0:T(1024)} %param.9) | copy-start | bytes 49156

commit v3 on v2

--- a/solution.py
+++ b/solution.py
@@ -22,8 +22,9 @@
 def kernel(
     sizes, q_hbm, k_hbm, v_hbm, ld_ref, gain_ref, out_ref,
     q_ref, k_ref, v_ref, cum, decay_cols, tail_cols, head_cols, bias, inner,
-    made, got1, t1, wsend, got2, t2, got3, t3, gsend, got4, csend, carried,
-    load_sem, send_sem, recv_sem, tsend_sem, trecv_sem,
+    made, pair, chip, got1, t1, wsend, got2, t2, made3, sums3, got3, t3, gsend, got4, csend, got5,
+    other, carried,
+    enter3, load_sem, send_sem, recv_sem, tsend_sem, trecv_sem, zsend_sem, zrecv_sem,
 ):
     narrow, depth, rows, heads, width, unit = sizes
     tokens = q_ref.shape[0]
@@ -31,11 +32,18 @@
     chunks = own // rows
     o, n = lax.axis_index("outer"), lax.axis_index("narrow")
     z, y = o // rows, lax.rem(o, rows)
+    chips = narrow // 2
+    x, core = n // 2, lax.rem(n, 2)
+    levels = depth.bit_length() - 1
 
     near = [lax.rem(n + i % narrow, narrow) for i in range(narrow // 2, narrow // 2 + narrow) if i % narrow]
+    partner = [1 - core]
+    across = [lax.rem(x + i, chips) for i in range(1, chips)]
     level = [lax.rem(y + i, rows) for i in range(1, rows)]
     deep = [lax.rem(z + i, depth) for i in range(1, depth)]
     group_at = lambda j: (o, j)
+    core_at = lambda j: (o, x * 2 + j)
+    chip_at = lambda j: (o, j * 2 + core)
     row_at = lambda j: (z * rows + j, n)
     depth_at = lambda j: (j * rows + y, n)
 
@@ -73,21 +81,22 @@
     def lanes(h):
         return pl.ds(pl.multiple_of(h * width, width), width)
 
-    def states(c):
-        def body(j, _):
+    def states(c, side):
+        def body(i, _):
             for r in range(rows):
                 k = c * rows + r
+                j = i * 2 + side
                 at = lanes(j * own + k)
                 tails = tail_cols[j * (own // unit) + k // unit]
                 u = k % unit
                 kept = k_ref[:, at].astype(jnp.float32) * tails[:, u : u + 1]
-                made[c, j, r] = lax.dot_general(
+                made[c, side, i, r] = lax.dot_general(
                     kept.astype(jnp.bfloat16), v_ref[:, at], (((0,), (0,)), ((), ())),
                     preferred_element_type=jnp.float32,
-                ).astype(jnp.bfloat16)
+                )
             return 0
 
-        lax.fori_loop(0, narrow, body, 0, unroll=2)
+        lax.fori_loop(0, chips, body, 0, unroll=2)
 
     def within(first, last):
         def body(g, _):
@@ -106,13 +115,14 @@
 
         lax.fori_loop(first, last, body, 0)
 
-    def finish(c, j):
+    def finish(c, side, i):
+        j = i * 2 + side
         for r in range(rows):
             k = c * rows + r
             at = lanes(j * own + k)
             grow = head_cols[j * (own // unit) + k // unit]
             u = k % unit
-            read = jnp.dot(q_ref[:, at], carried[c, j, r], preferred_element_type=jnp.float32)
+            read = jnp.dot(q_ref[:, at], carried[c, side, i, r], preferred_element_type=jnp.float32)
             numer = inner[:, at] + read * grow[:, u : u + 1]
             mean = jnp.mean(numer * numer, axis=-1, keepdims=True)
             out_ref[:, at] = (numer * lax.rsqrt(mean + 1e-06) * gain_ref[:, at]).astype(jnp.bfloat16)
@@ -154,62 +164,127 @@
     def decay(ref, j, k):
         return jnp.exp(ref[j, pl.ds(n * own + k, 1), :])
 
+    def decay_chip(j, k):
+        at = pl.ds(n * own + k, 1)
+        return jnp.exp(t1[j * 2, at, :] + t1[j * 2 + 1, at, :])
+
     def stage0(c):
-        states(c)
-        begin(0, c, lambda j: made.at[c, j], lambda j: got1.at[c, j], near, group_at, n)
-        got1[c, n] = made[c, n]
+        states(c, 1 - core)
+        begin(0, c, lambda j: made.at[c, j], lambda j: pair.at[c, j], partner, core_at, core)
+        states(c, core)
+        pair[c, core] = made[c, core]
 
     def stage1(c):
-        arrive(0, c, lambda j: got1.at[c, j], near, group_at)
+        arrive(0, c, lambda j: pair.at[c, j], partner, core_at)
+        for i in range(chips):
+            for r in range(rows):
+                at = pl.ds((i * 2 + core) * own + c * rows + r, 1)
+                acc = jnp.exp(t1[x * 2 + 1, at, :]) * pair[c, 0, i, r] + pair[c, 1, i, r]
+                chip[c, i, r] = acc.astype(chip.dtype)
+        begin(1, c, lambda j: chip.at[c, j], lambda j: got1.at[c, j], across, chip_at, x)
+        got1[c, x] = chip[c, x]
+
+    def stage2(c):
+        arrive(1, c, lambda j: got1.at[c, j], across, chip_at)
         for r in range(rows):
             acc = got1[c, 0, r].astype(jnp.float32)
-            for j in range(1, narrow):
-                acc = decay(t1, j, c * rows + r) * acc + got1[c, j, r].astype(jnp.float32)
-            wsend[c, r] = acc.astype(jnp.bfloat16)
-        begin(1, c, lambda j: wsend.at[c, j], lambda j: got2.at[c, j], level, row_at, y)
+            for j in range(1, chips):
+                acc = decay_chip(j, c * rows + r) * acc + got1[c, j, r].astype(jnp.float32)
+            wsend[c, r] = acc.astype(wsend.dtype)
+        begin(2, c, lambda j: wsend.at[c, j], lambda j: got2.at[c, j], level, row_at, y)
         got2[c, y] = wsend[c, y]
 
-    def stage2(c):
-        arrive(1, c, lambda j: got2.at[c, j], level, row_at)
+    def sender(l):
+        return lax.rem(z, 2 << l) == (1 << l) - 1
+
+    def receiver(l):
+        return lax.rem(z, 2 << l) >= (1 << l)
+
+    def depth_copy(c, l, i, to):
+        return pltpu.make_async_remote_copy(
+            src_ref=made3.at[c, l], dst_ref=got3.at[c, l], send_sem=zsend_sem.at[c, l, i],
+            recv_sem=zrecv_sem.at[c, l], device_id=depth_at(to), device_id_type=MESH,
+        )
+
+    def depth_send(c, l):
+        @pl.when(sender(l))
+        def _():
+            made3[c, l] = sums3[c].astype(made3.dtype)
+            for i in range(1 << l):
+                depth_copy(c, l, i, lax.rem(z + 1 + i, depth)).start()
+
+    def depth_take(c, l):
+        k = c * rows + y
+
+        @pl.when(receiver(l))
+        def _():
+            depth_copy(c, l, 0, lax.rem(z + depth - 1, depth)).wait_recv()
+            gap = jnp.zeros((1, width), jnp.float32)
+            for j in range(depth):
+                inside = jnp.logical_and(j >= z - lax.rem(z, 1 << l), j <= z)
+                gap = gap + jnp.where(inside, t3[j, pl.ds(n * own + k, 1), :], 0.0)
+            new = got3[c, l].astype(jnp.float32)
+            sums3[c] = jnp.exp(gap) * new + sums3[c]
+            before = gap - t3[z, pl.ds(n * own + k, 1), :]
+            enter3[c] = jnp.exp(before) * new + enter3[c]
+
+    def stage3(c):
+        arrive(2, c, lambda j: got2.at[c, j], level, row_at)
         acc = got2[c, 0].astype(jnp.float32)
         for j in range(1, rows):
             acc = decay(t2, j, c * rows + y) * acc + got2[c, j].astype(jnp.float32)
-        got3[c, z] = acc.astype(jnp.bfloat16)
-        begin(2, c, lambda j: got3.at[c, z], lambda j: got3.at[c, j], deep, depth_at, z)
-
-    def stage3(c):
-        arrive(2, c, lambda j: got3.at[c, j], deep, depth_at)
+        sums3[c] = acc
+        enter3[c] = jnp.zeros((width, width), jnp.float32)
+        depth_send(c, 0)
+
+    def stage4(c, l):
+        depth_take(c, l)
+        if l < levels - 1:
+            depth_send(c, l + 1)
+            return
         k = c * rows + y
-        acc = jnp.zeros((width, width), jnp.float32)
-        for j in range(depth - 1):
-            new = decay(t3, j, k) * acc + got3[c, j].astype(jnp.float32)
-            acc = jnp.where(j < z, new, acc)
+        acc = enter3[c]
         for j in range(rows):
-            gsend[c, j] = acc.astype(jnp.bfloat16)
+            gsend[c, j] = acc.astype(gsend.dtype)
             if j < rows - 1:
                 acc = decay(t2, j, k) * acc + got2[c, j].astype(jnp.float32)
         begin(3, c, lambda j: gsend.at[c, j], lambda j: got4.at[c, j], level, row_at, y)
         got4[c, y] = gsend[c, y]
 
-    def stage4(c):
+    def stage5(c):
         arrive(3, c, lambda j: got4.at[c, j], level, row_at)
         for r in range(rows):
             acc = got4[c, r].astype(jnp.float32)
-            for j in range(narrow):
-                csend[c, j, r] = acc.astype(jnp.bfloat16)
-                if j < narrow - 1:
-                    acc = decay(t1, j, c * rows + r) * acc + got1[c, j, r].astype(jnp.float32)
-        begin(4, c, lambda j: csend.at[c, j], lambda j: carried.at[c, j], near, group_at, n)
-        carried[c, n] = csend[c, n]
-
-    def stage5(c):
-        arrive(4, c, lambda j: carried.at[c, j], near, group_at)
-
-        def body(j, _):
-            finish(c, j)
+            for j in range(chips):
+                csend[c, j, r] = acc.astype(csend.dtype)
+                if j < chips - 1:
+                    acc = decay_chip(j, c * rows + r) * acc + got1[c, j, r].astype(jnp.float32)
+        begin(4, c, lambda j: csend.at[c, j], lambda j: got5.at[c, j], across, chip_at, x)
+        got5[c, x] = csend[c, x]
+
+    def stage6(c):
+        arrive(4, c, lambda j: got5.at[c, j], across, chip_at)
+        for i in range(chips):
+            for r in range(rows):
+                at = pl.ds((i * 2 + core) * own + c * rows + r, 1)
+                first = got5[c, i, r]
+                later = jnp.exp(t1[x * 2, at, :]) * first.astype(jnp.float32) + pair[c, 0, i, r]
+                first = first.astype(jnp.float32)
+                other[c, i, r] = jnp.where(core == 0, later, first).astype(other.dtype)
+                carried[c, core, i, r] = jnp.where(core == 0, first, later).astype(carried.dtype)
+        begin(5, c, lambda j: other.at[c], lambda j: carried.at[c, core], partner, core_at, core)
+        finish_side(c, core)
+
+    def finish_side(c, side):
+        def body(i, _):
+            finish(c, side, i)
             return 0
 
-        lax.fori_loop(0, narrow, body, 0, unroll=2)
+        lax.fori_loop(0, chips, body, 0, unroll=2)
+
+    def stage7(c):
+        arrive(5, c, lambda j: carried.at[c, j], partner, core_at)
+        finish_side(c, 1 - core)
 
     def totals1():
         arrive_total(0, t1, near, group_at)
@@ -237,31 +312,41 @@
     loads[2].wait()
 
     groups = heads // unit
-    events = [(TIMES[p] + GAP * c, p, c) for p in range(5) for c in range(chunks)]
-    events += [(TIMES[1] - 0.1, 5, 0), (TIMES[2] - 0.1, 6, 0)]
+    slots = [stage1, stage2, stage3]
+    slots += [functools.partial(lambda l, c: stage4(c, l), l) for l in range(levels)]
+    slots += [stage5, stage6, stage7]
+    gaps = STEPS[:3] + (STEPS[3],) * levels + STEPS[4:]
+    times = [sum(gaps[: p + 1]) for p in range(len(slots))]
+    events = [(times[p] + GAP * c, p, c) for p in range(len(slots)) for c in range(chunks)]
     early = min(groups, EARLY)
     within(0, early)
     filled = early
     for _, p, c in sorted(events):
-        if p == 4 and filled < groups:
+        if slots[p] is stage6 and filled < groups:
             within(filled, groups)
             filled = groups
-        if p == 5:
+        if slots[p] is stage3 and c == 0:
             totals2()
-        elif p == 6:
+        if p == 3 and c == 0:
             arrive_total(2, t3, deep, depth_at)
-        else:
-            (stage1, stage2, stage3, stage4, stage5)[p](c)
-            if filled < groups:
-                within(filled, filled + 1)
-                filled += 1
+        slots[p](c)
+        if filled < groups:
+            within(filled, filled + 1)
+            filled += 1
     for one in pending:
         one.wait_send()
-
-
-TIMES = (5.4, 7.8, 12.8, 15.2, 19.6)
-GAP = 2.75
-EARLY = 2
+    for l in range(levels):
+
+        @pl.when(sender(l))
+        def _():
+            for c in range(chunks):
+                for i in range(1 << l):
+                    depth_copy(c, l, i, lax.rem(z + 1 + i, depth)).wait_send()
+
+
+STEPS = (2.5, 3.0, 2.3, 2.4, 2.3, 3.0, 1.5)
+GAP = 1.6
+EARLY = 0
 
 
 def on_device(mesh_sizes, queries, keys, values, log_decay, gain):
@@ -274,6 +359,9 @@
     chunks = own // rows
     unit = min(4, own)
     half = lambda *shape: pltpu.VMEM(shape + (width, width), jnp.bfloat16)
+    wide = lambda *shape: pltpu.VMEM(shape + (width, width), jnp.float32)
+    chips = narrow // 2
+    levels = depth.bit_length() - 1
     full = lambda *shape: pltpu.VMEM(shape, jnp.float32)
     most = max(narrow, depth, rows)
     dma = lambda *shape: pltpu.SemaphoreType.DMA(shape)
@@ -294,26 +382,35 @@
             full(heads // unit, tokens, 128),
             full(tokens, tokens),
             full(tokens, model),
-            half(chunks, narrow, rows),
-            half(chunks, narrow, rows),
+            wide(chunks, 2, chips, rows),
+            wide(chunks, 2, chips, rows),
+            half(chunks, chips, rows),
+            half(chunks, chips, rows),
             full(narrow, heads, width),
             half(chunks, rows),
             half(chunks, rows),
             full(rows, heads, width),
-            half(chunks, depth),
+            half(chunks, levels),
+            wide(chunks),
+            half(chunks, levels),
             full(depth, heads, width),
             half(chunks, rows),
             half(chunks, rows),
-            half(chunks, narrow, rows),
-            half(chunks, narrow, rows),
+            half(chunks, chips, rows),
+            half(chunks, chips, rows),
+            half(chunks, chips, rows),
+            half(chunks, 2, chips, rows),
+            wide(chunks),
             dma(3),
-            dma(5, chunks, most),
-            dma(5, chunks, most),
+            dma(6, chunks, most),
+            dma(6, chunks, most),
             dma(3, most),
             dma(3, most),
+            dma(chunks, levels, depth),
+            dma(chunks, levels),
         ],
         compiler_params=pltpu.CompilerParams(
-            collective_id=0, has_side_effects=True, vmem_limit_bytes=48 * 1024 * 1024
+            collective_id=0, has_side_effects=True, vmem_limit_bytes=60 * 1024 * 1024
         ),
     )(queries, keys, values, log_decay, gain.reshape(1, model))
 

time: 43.1 us -> 43.4 us (level); the launches traced: 42.8 us -> 42.7 us
  local copies, waits for them, and re-layouts: 4.39 us -> 3.13 us
  Pallas kernels: 38.4 us -> 39.5 us
    unnamed x7 -> x1, local copies, waits for them, and re-layouts: 4.39 us -> 3.13 us
    pallas_call x1, Pallas kernels: 38.4 us -> 39.5 us  [on_device(): pl.pallas_call(functools.partial(kernel, (narrow, depth, rows, heads, wid...]
where the time goes in v3:
time: 43.4 us; the launch traced here: 42.7 us
  Pallas kernels  39.5 us (91%)
  local copies, waits for them, and re-layouts  3.13 us (7%)
    pallas_call x1, Pallas kernels, on_device(): pl.pallas_call(functools.partial(kernel, (narrow, depth, rows, heads, wid...  39.5 us
    unnamed x1, local copies, waits for them, and re-layouts  3.13 us

profile of v3, /device:TPU:1, one launch (start us, length us, event | category | flops | bytes accessed | tf_op | source)
XLA Modules:
  0.0 42.7 jit_solution(2565759660344394258)
XLA Ops:
  0.0 39.5 %shard_map.55 = bf16[256,4096]{1,0:T(8,128)(2,1)} custom-call(bf16[256,4096]{1,0:T(8,128)(2,1)} %q_hbm.1, bf16[256,4096]{1,0:T(8,128)(2,1)} %k_hbm.1, bf16[256,4096]{1,0:T(8,128)(2,1)} %v_hbm.1, f32[32,256]{1,0:T(8,128)} %ld_ref.1, f32[1,4096]{1,0:T(1,128)} %bitcast.1), custom_call_target="tpu_custom_call" | custom-call | tf_op jit(solution)/shard_map/pallas_call | solution.py:370
  39.5 3.1 %copy.7 = bf16[256,4096]{1,0:T(8,128)(2,1)} copy(bf16[256,4096]{1,0:T(8,128)(2,1)} %shard_map.55) | data formatting | bytes 4194304

commit v4 on v2

--- a/solution.py
+++ b/solution.py
@@ -261,7 +261,7 @@
 
 TIMES = (5.4, 7.8, 12.8, 15.2, 19.6)
 GAP = 2.75
-EARLY = 2
+EARLY = 0
 
 
 def on_device(mesh_sizes, queries, keys, values, log_decay, gain):
@@ -313,7 +313,7 @@
             dma(3, most),
         ],
         compiler_params=pltpu.CompilerParams(
-            collective_id=0, has_side_effects=True, vmem_limit_bytes=48 * 1024 * 1024
+            collective_id=0, has_side_effects=True, vmem_limit_bytes=60 * 1024 * 1024
         ),
     )(queries, keys, values, log_decay, gain.reshape(1, model))
 

time: 43.1 us -> 43.4 us (level)
  Pallas kernels: 38.4 us -> 40.1 us
  local copies, waits for them, and re-layouts: 4.39 us -> 3.13 us
    pallas_call x1, Pallas kernels: 38.4 us -> 40.1 us  [on_device(): pl.pallas_call(functools.partial(kernel, (narrow, depth, rows, heads, wid...]
    unnamed x7 -> x1, local copies, waits for them, and re-layouts: 4.39 us -> 3.13 us
where the time goes in v4:
time: 43.4 us; the launch traced here: 43.2 us
  Pallas kernels  40.1 us (92%)
  local copies, waits for them, and re-layouts  3.13 us (7%)
    pallas_call x1, Pallas kernels, on_device(): pl.pallas_call(functools.partial(kernel, (narrow, depth, rows, heads, wid...  40.1 us
    unnamed x1, local copies, waits for them, and re-layouts  3.13 us

profile of v4, /device:TPU:1, one launch (start us, length us, event | category | flops | bytes accessed | tf_op | source)
XLA Modules:
  0.0 43.2 jit_solution(1246964433700443305)
XLA Ops:
  0.0 40.1 %shard_map.55 = bf16[256,4096]{1,0:T(8,128)(2,1)} custom-call(bf16[256,4096]{1,0:T(8,128)(2,1)} %q_hbm.1, bf16[256,4096]{1,0:T(8,128)(2,1)} %k_hbm.1, bf16[256,4096]{1,0:T(8,128)(2,1)} %v_hbm.1, f32[32,256]{1,0:T(8,128)} %ld_ref.1, f32[1,4096]{1,0:T(1,128)} %bitcast.1), custom_call_target="tpu_custom_call" | custom-call | tf_op jit(solution)/shard_map/pallas_call | solution.py:282
  40.1 3.1 %copy.7 = bf16[256,4096]{1,0:T(8,128)(2,1)} copy(bf16[256,4096]{1,0:T(8,128)(2,1)} %shard_map.55) | data formatting | bytes 4194304
